TPU v7x, 32 devices: a whole 2x2x4 slice. The times are simulated.
32 devices in a mesh: row: 8 (over z, y), col: 4 (over x, core).
Axes of the slice: x: 2, y: 2, z: 4, core: 2. Of those that a mesh axis runs over, the one named last changes fastest.
Arguments:
- leaf_inverse: bfloat16 [32, 1024, 1024], P(('row', 'col')), as said below
- leaf_rhs: bfloat16 [32, 1024, 512], P(('row', 'col')), may hold values from -6 to 6
- leaf_tiles: bfloat16 [32, 1024, 1024], P(('row', 'col')), may hold values from -0.09375 to 0.09375
- mid_inverse_t: bfloat16 [8, 1024, 1024], P('col', None, 'row'), as said below
- mid_rhs: bfloat16 [8, 1024, 512], P('col', 'row'), may hold values from -6 to 6
- mid_tiles: bfloat16 [8, 1024, 1024], P('col', None, 'row'), may hold values from -0.125 to 0.125
- top_inverse_t: bfloat16 [2, 1024, 1024], P(None, None, 'col'), as said below
- top_rhs: bfloat16 [2, 1024, 512], P(None, 'col'), may hold values from -6 to 6
- tile_lists: int32 [32, 1], P(('row', 'col')), may hold values from 0 to 1
Outputs:
- leaf_solved: bfloat16 [32, 1024, 512], P(('row', 'col'))
- mid_solved: bfloat16 [8, 1024, 512], P('col', 'row')
- top_solved: bfloat16 [2, 1024, 512], P(None, 'col')
Inputs may be any that keep to these rules, and one draw needn't show every extreme that they name: Each leaf_inverse[d] is zero above its diagonal and has diagonal entries between 0.75 and 1.25. Each mid_inverse_t[q] is zero below its diagonal and has diagonal entries between 0.75 and 1.25. Each top_inverse_t[b] is zero below its diagonal and has diagonal entries between 0.75 and 1.25.
All inputs are finite; a program needn't handle non-finite values.
Results may differ from a plain program's by a relative error of at most 0.0065.
Values may be sent and summed in bfloat16 or wider, within the bound.
No kernel may reach another device: no remote copies, remote signals or barrier semaphores. Data moves between devices by JAX's collectives and lax.ppermute only.
A program may use at most 64 MiB of HBM per device.

v0:
```python
import jax
import jax.numpy as jnp
from jax import lax
from jax.sharding import PartitionSpec as P

NB = 2


def solve_piece(inverse_cols, piece):
    return lax.dot_general(
        inverse_cols, piece, (((1,), (1,)), ((0,), (0,))), preferred_element_type=jnp.float32
    )


def local(
    leaf_inverse,
    leaf_rhs,
    leaf_tiles,
    mid_inverse_t,
    mid_rhs,
    mid_tiles,
    top_inverse_t,
    top_rhs,
    tile_lists,
):
    slot_ids = jnp.arange(NB, dtype=jnp.int32)[:, None, None]
    solved_leaf = jnp.dot(leaf_inverse[0], leaf_rhs[0], preferred_element_type=jnp.float32).astype(
        jnp.bfloat16
    )
    leaf_update = jnp.dot(leaf_tiles[0], solved_leaf, preferred_element_type=jnp.float32)
    mid_terms = jnp.where(slot_ids == tile_lists[0, 0], leaf_update[None], 0.0)
    mid_share = lax.psum_scatter(mid_terms, "row", scatter_dimension=1, tiled=True)
    mid_resid = (mid_rhs.astype(jnp.float32) - mid_share).astype(jnp.bfloat16)
    mid_own = solve_piece(
        mid_inverse_t, lax.all_gather(mid_resid, "row", axis=1, tiled=True)
    ).astype(jnp.bfloat16)
    top_terms = lax.dot_general(
        mid_tiles, mid_own, (((2,), (1,)), ((0,), (0,))), preferred_element_type=jnp.float32
    )
    summed_rows = lax.psum(top_terms, "row")
    top_share = lax.psum_scatter(summed_rows, "col", scatter_dimension=1, tiled=True)
    top_resid = (top_rhs.astype(jnp.float32) - top_share).astype(jnp.bfloat16)
    top_own = solve_piece(
        top_inverse_t, lax.all_gather(top_resid, "col", axis=1, tiled=True)
    ).astype(jnp.bfloat16)
    return (solved_leaf[None], mid_own, top_own)


def solution(mesh):
    placed = (
        P(("row", "col"), None, None),
        P(("row", "col"), None, None),
        P(("row", "col"), None, None),
        P("col", None, "row"),
        P("col", "row", None),
        P("col", None, "row"),
        P(None, None, "col"),
        P(None, "col", None),
        P(("row", "col"), None),
    )
    return jax.shard_map(
        local,
        mesh=mesh,
        in_specs=placed,
        out_specs=(P(("row", "col"), None, None), P("col", "row", None), P(None, "col", None)),
        check_vma=False,
    )
```

profile of v0, /device:TPU:0, one launch (start us, length us, event | category | flops | bytes accessed | tf_op | source)
XLA Modules:
  0.0 324.7 jit_solution(155862839401762226)
XLA Ops:
  7.2 0.0 copy-start
  7.2 0.0 reduce-scatter.3.cloned.1.call-start
  8.0 0.8 copy-done
  8.8 0.0 copy-start.4
  8.8 2.6 fusion.7
  11.4 0.0 copy-start.5
  11.4 1.0 copy-done.5
  12.4 0.0 copy-done.4
  12.4 1.3 fusion.4
  13.7 2.5 broadcast_select_fusion
  16.2 0.0 copy-start.3
  16.2 0.0 reduce-scatter.3.cloned.1.call-update
  16.2 0.0 all-gather.3.cloned.1.call-start
  16.3 0.9 copy-done.3
  17.2 0.2 copy.12
  17.3 0.0 copy-start.1
  17.4 90.4 %reduce-scatter.3.cloned.1.call-done = f32[2,128,512]{1,2,0:T(8,128)} async-done(((f32[2,1024,512]{1,2,0:T(8,128)}), f32[2,128,512]{1,2,0:T(8,128)}) %reduce-scatter.3.cloned.1.call-update) | async-done | bytes 524304 | tf_op jit(solution)/shard_map/reduce_scatter | solution.py:32
  107.8 1.8 subtract_convert_fusion.1
  109.6 0.0 all-gather.3.cloned.1.call-update
  109.6 0.0 reduce-scatter.5.cloned.1.call-start
  109.7 50.8 %all-gather.3.cloned.1.call-done = bf16[2,1024,512]{1,2,0:T(8,128)(2,1)} async-done(((bf16[2,128,512]{1,2,0:T(8,128)(2,1)}), bf16[2,1024,512]{1,2,0:T(8,128)(2,1)}) %all-gather.3.cloned.1.call-update) | async-done | bytes 2097168 | tf_op jit(solution)/shard_map/all_gather | solution.py:35
  160.4 2.4 convolution_convert_fusion.1
  162.8 0.0 copy-done.1
  162.8 2.7 convolution_bitcast_fusion
  165.5 0.0 copy-start.2
  165.5 0.0 reduce-scatter.5.cloned.1.call-update
  165.5 0.0 all-reduce.2.cloned.1.call-start
  165.5 42.7 %reduce-scatter.5.cloned.1.call-done = f32[2,256,512]{1,2,0:T(8,128)} async-done(((f32[2,1024,512]{1,2,0:T(8,128)}), f32[2,256,512]{1,2,0:T(8,128)}) %reduce-scatter.5.cloned.1.call-update) | async-done | bytes 1048592 | tf_op jit(solution)/shard_map/reduce_scatter | solution.py:41
  208.2 0.0 all-reduce.2.cloned.1.call-update
  208.3 0.0 all-gather.5.cloned.1.call-start
  208.3 0.0 copy-done.2
  208.3 0.2 copy.13
  208.5 81.3 %all-reduce.2.cloned.1.call-done = f32[2,256,512]{1,2,0:T(8,128)} async-done(((f32[2,256,512]{1,2,0:T(8,128)}), f32[2,256,512]{1,2,0:T(8,128)}) %all-reduce.2.cloned.1.call-update) | async-done | bytes 1048592 | tf_op jit(solution)/shard_map/psum | solution.py:40
  289.8 2.1 subtract_convert_fusion
  292.0 0.0 all-gather.5.cloned.1.call-update
  292.0 0.9 copy.14
  292.8 21.7 %all-gather.5.cloned.1.call-done = bf16[2,1024,512]{1,2,0:T(8,128)(2,1)} async-done(((bf16[2,256,512]{1,2,0:T(8,128)(2,1)}), bf16[2,1024,512]{1,2,0:T(8,128)(2,1)}) %all-gather.5.cloned.1.call-update) | async-done | bytes 2097168 | tf_op jit(solution)/shard_map/all_gather | solution.py:44
  314.6 2.6 fusion.10
  317.1 1.0 copy.15
  (1 shorter events, 0.0 us)
Async XLA Ops:
  7.2 1.6 copy-start
  7.2 100.6 %reduce-scatter.3.cloned.1.call-start = ((), (), s32[]{:S(2)}) async-start(), calls=%async_computation.2 | async-start | bytes 4718592 | tf_op jit(solution)/shard_map/reduce_scatter | solution.py:32
  8.8 3.6 %copy-start.4 = (bf16[1,1024,1024]{2,1,0:T(8,128)(2,1)S(1)}, bf16[1,1024,1024]{2,1,0:T(8,128)(2,1)}, u32[]{:S(2)}) copy-start(bf16[1,1024,1024]{2,1,0:T(8,128)(2,1)} %param.11) | copy-start | bytes 6291460
  11.4 1.0 copy-start.5
  16.2 0.9 copy-start.3
  16.2 144.2 %all-gather.3.cloned.1.call-start = ((), (), s32[]{:S(2)}) async-start(), calls=%async_computation.3 | async-start | bytes 2359296 | tf_op jit(solution)/shard_map/all_gather | solution.py:35
  17.3 145.5 %copy-start.1 = (bf16[2,1024,128]{2,1,0:T(8,128)(2,1)S(1)}, bf16[2,1024,128]{2,1,0:T(8,128)(2,1)}, u32[]{:S(2)}) copy-start(bf16[2,1024,128]{2,1,0:T(8,128)(2,1)} %param.14) | copy-start | bytes 1572868
  109.6 98.6 %reduce-scatter.5.cloned.1.call-start = ((), (), s32[]{:S(2)}) async-start(), calls=%async_computation.5 | async-start | bytes 5242880 | tf_op jit(solution)/shard_map/reduce_scatter | solution.py:41
  165.5 42.8 %copy-start.2 = (bf16[2,256,512]{2,1,0:T(8,128)(2,1)S(1)}, bf16[2,256,512]{2,1,0:T(8,128)(2,1)}, u32[]{:S(2)}) copy-start(bf16[2,256,512]{2,1,0:T(8,128)(2,1)} %param.16) | copy-start | bytes 1572868
  165.5 124.3 %all-reduce.2.cloned.1.call-start = ((), (), s32[]{:S(2)}) async-start(), calls=%async_computation.6 | async-start | bytes 2097152 | tf_op jit(solution)/shard_map/psum | solution.py:40
  208.3 106.3 %all-gather.5.cloned.1.call-start = ((), (), s32[]{:S(2)}) async-start(), calls=%async_computation.4 | async-start | bytes 2621440 | tf_op jit(solution)/shard_map/all_gather | solution.py:44
Sparse Core Ops, SparseCore 0:
  16.4 91.3 reduce-scatter.2
  110.4 49.9 all-gather.2
  165.6 42.5 reduce-scatter.4
  211.6 78.1 all-reduce.1
  292.1 22.3 all-gather.4
where the time goes:
time: 325 us
  waiting for transfers between devices  287 us (88%)
  between operations  14.6 us (4%)
  matrix products  11.5 us (4%)
  other arithmetic  6.48 us (2%)
  local copies, waits for them, and re-layouts  4.84 us (1%)
    reduce_scatter x1, waiting for transfers between devices, local(): lax.psum_scatter(mid_terms, 'row', scatter_dimension=1, tiled=True)  90.4 us
    psum x1, waiting for transfers between devices, local(): summed_rows = lax.psum(top_terms, 'row')  81.3 us
    all_gather x1, waiting for transfers between devices, local(): lax.all_gather(mid_resid, 'row', axis=1, tiled=True)  50.8 us
    reduce_scatter x1, waiting for transfers between devices, local(): lax.psum_scatter(summed_rows, 'col', scatter_dimension=1, tiled=True)  42.7 us
    all_gather x1, waiting for transfers between devices, local(): lax.all_gather(top_resid, 'col', axis=1, tiled=True)  21.7 us
  transfers between devices with their start and end apart: 5, of which 5 were waited for; matrix products, arithmetic and copies ran while one was open for 0% of the time, Pallas kernels for 0%

commit v1 on v0

v1 whole, which is shorter than its diff:
```python
import jax
import jax.numpy as jnp
from jax import lax
from jax.experimental import pallas as pl
from jax.experimental.pallas import tpu as pltpu
from jax.sharding import PartitionSpec as P


CORES = 2
MARK = 16
LANES = 128


F32, BF16 = jnp.float32, jnp.bfloat16
VMEM = pl.BlockSpec(memory_space=pltpu.VMEM)
SMEM = pl.BlockSpec(memory_space=pltpu.SMEM)
HBM = pl.BlockSpec(memory_space=pltpu.HBM)


def wide(x):
    return x.astype(F32)


def total(terms):
    acc = terms[0]
    for term in terms[1:]:
        acc = acc + term
    return acc


def dot(a, b, a_dim):
    return lax.dot_general(a, b, (((a_dim,), (0,)), ((), ())), preferred_element_type=F32)


def in_hbm(x):
    return pltpu.with_memory_space_constraint(x, pltpu.HBM)


def call(body, shapes, args, specs=None, scratch=(), out_specs=None):
    return pl.pallas_call(
        body,
        out_shape=[jax.ShapeDtypeStruct(s, BF16) for s in shapes],
        in_specs=specs or [VMEM] * len(args),
        out_specs=out_specs or [VMEM] * len(shapes),
        scratch_shapes=scratch,
        compiler_params=pltpu.CompilerParams(vmem_limit_bytes=16 << 20),
    )(*args)


def leaf_stage(leaf_inverse, leaf_rhs, leaf_tiles, tile_lists, mid_inverse_t, mid_tiles, n_row):
    nb, _, own_rows = mid_inverse_t.shape
    depth, src = leaf_rhs.shape
    rows = depth // n_row
    chunks = src // LANES
    step = min(256, depth)

    count = depth // step

    def body(inverse_hbm, rhs_hbm, tiles_hbm, slot, mid_inverse, mid_tile, solved_hbm, swap, *rest):
        blocks = rest[:n_row]
        inverse, rhs, tiles, solved, update, sems = rest[n_row:]
        row = lax.axis_index("row")
        spans = [slice(i * step, (i + 1) * step) for i in range(count)]

        def fetch(source, target, sem, *at):
            copy = pltpu.make_async_copy(source.at[at], target.at[at], sem)
            copy.start()
            return copy

        first, second = [], []
        for i, span in enumerate(spans):
            first.append(fetch(rhs_hbm, rhs, sems.at[0, i], span))
            first.append(
                fetch(inverse_hbm, inverse, sems.at[1, i], span, slice(0, (i + 1) * step))
            )
        for i, span in enumerate(spans):
            second.append(fetch(tiles_hbm, tiles, sems.at[2, i], span))
        stored = []
        for i, source in enumerate((mid_inverse, mid_tile)):
            copy = pltpu.make_async_copy(source.at[1 - row % nb], swap.at[i], sems.at[4, i])
            copy.start()
            stored.append(copy)
        for i, span in enumerate(spans):
            first[2 * i].wait()
            first[2 * i + 1].wait()
            block = dot(inverse[span, : (i + 1) * step], rhs[: (i + 1) * step, :], 1)
            solved[span, :] = block.astype(BF16)
            copy = pltpu.make_async_copy(solved.at[span], solved_hbm.at[span], sems.at[3, i])
            copy.start()
            stored.append(copy)
        for i, span in enumerate(spans):
            second[i].wait()
            update[span, :] = dot(tiles[span, :], solved[...], 1).astype(BF16)
        mark = jnp.full((MARK, LANES), slot[0, 0].astype(F32), F32).astype(BF16)
        for k in range(n_row):
            at = pl.ds(pl.multiple_of((row ^ k) * rows, rows), rows)
            for j in range(chunks):
                lanes = slice(j * LANES, (j + 1) * LANES)
                blocks[k][j * rows : (j + 1) * rows, :] = update[at, lanes]
            blocks[k][chunks * rows :, :] = mark
        for copy in stored:
            copy.wait()

    out = call(
        body,
        [(depth, src), (2, depth, own_rows)] + [(chunks * rows + MARK, LANES)] * n_row,
        (
            *map(in_hbm, (leaf_inverse, leaf_rhs, leaf_tiles)),
            tile_lists,
            *map(in_hbm, (mid_inverse_t, mid_tiles)),
        ),
        [HBM, HBM, HBM, SMEM, HBM, HBM],
        [
            pltpu.VMEM((depth, depth), BF16),
            pltpu.VMEM((depth, src), BF16),
            pltpu.VMEM((depth, depth), BF16),
            pltpu.VMEM((depth, src), BF16),
            pltpu.VMEM((depth, src), BF16),
            pltpu.SemaphoreType.DMA((5, max(count, 2))),
        ],
        [HBM] + [VMEM] * (n_row + 1),
    )
    return out[0], out[1], out[2:]


def slot_sums(blocks, nb, rows, chunk):
    sums = [None] * nb
    for ref in blocks:
        value = wide(ref[chunk * rows : (chunk + 1) * rows, :])
        mark = wide(ref[ref.shape[0] - MARK : ref.shape[0] - MARK + 1, :])
        for s in range(nb):
            term = jnp.where(mark == float(s), value, 0.0)
            sums[s] = term if sums[s] is None else sums[s] + term
    return sums


def cross_stage(blocks, nb, rows, src):
    def body(*refs):
        outs = refs[len(blocks) :]
        for j in range(src // LANES):
            sums = slot_sums(refs[: len(blocks)], nb, rows, j)
            for s in range(nb):
                outs[0][s * rows : (s + 1) * rows, j * LANES : (j + 1) * LANES] = sums[s].astype(
                    BF16
                )

    return call(body, [(nb * rows, src)], tuple(blocks))[0]


def resid_stage(blocks, crossed, mid_rhs):
    nb, rows, src = mid_rhs.shape

    def body(*refs):
        near = refs[: len(blocks)]
        far, rhs, mine, other = refs[len(blocks) :]
        y = lax.axis_index("row") % nb
        for j in range(src // LANES):
            lanes = slice(j * LANES, (j + 1) * LANES)
            sums = slot_sums(near, nb, rows, j)
            first, second = [
                wide(rhs[s, :, lanes])
                - (sums[s] + wide(far[s * rows : (s + 1) * rows, lanes]))
                for s in range(nb)
            ]
            mine[:, lanes] = jnp.where(y == 0, first, second).astype(BF16)
            other[:, lanes] = jnp.where(y == 0, second, first).astype(BF16)

    return call(body, [(rows, src)] * nb, (*blocks, crossed, mid_rhs))


def mid_stage(blocks, mid_inverse_t, mid_tiles, swapped, n_x, own_top):
    nb, _, rows = mid_inverse_t.shape
    src = blocks[0][0].shape[1]
    n_z = len(blocks)

    def body(*refs):
        parts, (inverse, tiles, swap, own, other, sent) = refs[: 2 * n_z], refs[2 * n_z :]
        row, core = lax.axis_index("row"), lax.axis_index("col") % CORES
        z, y = row // nb, row % nb
        acc = None
        for i, ref in enumerate(parts):
            owner = ((z - i // 2 + n_z) % n_z) * nb + (y ^ (i % 2))
            at = pl.ds(pl.multiple_of(owner * rows, rows), rows)
            part = jnp.concatenate([inverse[y, at, :], swap[0, at, :]], axis=1)
            term = dot(part, ref[...], 0)
            acc = term if acc is None else acc + term
        solved = acc.astype(BF16)
        own[...] = solved[:rows]
        other[...] = solved[rows:]
        for x in range(n_x):
            at = pl.ds(pl.multiple_of((x * CORES + 1 - core) * own_top, own_top), own_top)
            part = jnp.concatenate([tiles[y, at, :], swap[1, at, :]], axis=1)
            sent[x] = dot(part, solved, 1).astype(BF16)

    return call(
        body,
        [(rows, src), (rows, src), (n_x, own_top, src)],
        (*[b for pair in blocks for b in pair], mid_inverse_t, mid_tiles, swapped),
    )


def core_stage(own, other, mid_tiles, swapped, got, n_z):
    n_x, own_top, src = got.shape
    nb = mid_tiles.shape[0]
    width = src // n_z
    dense = width % LANES == 0

    def body(own, other, tiles, swap, far, *rest):
        outs, part = (rest[:-1], rest[-1]) if dense else (None, rest[0])
        row, core = lax.axis_index("row"), lax.axis_index("col") % CORES
        z, y = row // nb, row % nb
        solved = jnp.concatenate([own[...], other[...]], axis=0)
        for x in range(n_x):
            at = pl.ds(pl.multiple_of((x * CORES + core) * own_top, own_top), own_top)
            tile = jnp.concatenate([tiles[y, at, :], swap[1, at, :]], axis=1)
            term = dot(tile, solved, 1) + wide(far[x])
            part[x * own_top : (x + 1) * own_top, :] = term.astype(BF16)
        for k in range(n_z if dense else 0):
            lanes = pl.ds(pl.multiple_of((z ^ k) * width, width), width)
            outs[k][...] = part[:, lanes]

    args = (own, other, mid_tiles, swapped, got)
    rows = n_x * own_top
    if dense:
        return call(body, [(rows, width)] * n_z, args, scratch=[pltpu.VMEM((rows, src), BF16)])
    part = call(body, [(rows, src)], args)[0]
    z = lax.axis_index("row") // nb
    return [lax.dynamic_slice_in_dim(part, (z ^ k) * width, width, 1) for k in range(n_z)]


def share_stage(top_rhs, n_z):
    n_top, rows, src = top_rhs.shape
    width = src // n_z
    row = lax.axis_index("row")
    if width % LANES:
        part = lax.dynamic_index_in_dim(top_rhs, row % n_top, 0, keepdims=False)
        return lax.dynamic_slice_in_dim(part, row // n_top * width, width, 1)

    def body(rhs, out):
        row = lax.axis_index("row")
        lanes = pl.ds(pl.multiple_of(row // n_top * width, width), width)
        out[...] = rhs[row % n_top, :, lanes]

    return call(body, [(rows, width)], (top_rhs,))[0]


def sum_stage(pieces):
    def body(*refs):
        refs[-1][...] = total([wide(ref[...]) for ref in refs[:-1]]).astype(BF16)

    return call(body, [pieces[0].shape], tuple(pieces))[0]


def top_resid_stage(pieces, shares):
    n_x = len(shares)
    rows, width = shares[0].shape

    def body(*refs):
        terms, rhs, out = refs[: len(pieces)], refs[len(pieces) : -1], refs[-1]
        x = lax.axis_index("col") // CORES
        for dx in range(n_x):
            at = pl.ds(pl.multiple_of((x ^ dx) * rows, rows), rows)
            update = total([wide(ref[at, :]) for ref in terms])
            out[at, :] = (wide(rhs[dx][...]) - update).astype(BF16)

    return call(body, [(n_x * rows, width)], (*pieces, *shares))[0]


def top_solve_stage(pieces, top_inverse_t):
    n_top, _, rows = top_inverse_t.shape
    width = pieces[0].shape[1]
    n_x = pieces[0].shape[0] // rows

    def body(*refs):
        parts, inverse, out = refs[:CORES], refs[CORES], refs[CORES + 1]
        y, core = lax.axis_index("row") % n_top, lax.axis_index("col") % CORES
        acc = None
        for k, ref in enumerate(parts):
            for x in range(n_x):
                start = pl.multiple_of((x * CORES + (core ^ k)) * rows, rows)
                part = ref[x * rows : (x + 1) * rows, :]
                term = dot(inverse[y, pl.ds(start, rows), :], part, 0)
                acc = term if acc is None else acc + term
        out[...] = acc.astype(BF16)

    return call(body, [(rows, width)], (*pieces, top_inverse_t))[0]


def spread_stage(pieces, n_z, n_top):
    rows, width = pieces[0].shape

    def body(*refs):
        out = refs[len(pieces)]
        row = lax.axis_index("row")
        for k, ref in enumerate(refs[: len(pieces)]):
            z, y = (row ^ k) // n_top, (row ^ k) % n_top
            out[y, :, pl.ds(pl.multiple_of(z * width, width), width)] = ref[...]

    return call(body, [(n_top, rows, n_z * width)], tuple(pieces))[0]


def narrow_spread(pieces, n_z, n_top):
    rows, width = pieces[0].shape
    row = lax.axis_index("row")
    out = jnp.zeros((n_z * n_top, rows, width), BF16)
    for k, piece in enumerate(pieces):
        out = lax.dynamic_update_index_in_dim(out, piece, row ^ k, 0)
    out = out.reshape(n_z, n_top, rows, width).transpose(1, 2, 0, 3)
    return out.reshape(n_top, rows, n_z * width)


def make_local(n_row, n_col):
    n_x = n_col // CORES
    half = n_row // 2

    def row_xor(x, k):
        return lax.ppermute(x, "row", [(i, i ^ k) for i in range(n_row)])

    def col_xor(x, k):
        return lax.ppermute(x, "col", [(i, i ^ k) for i in range(n_col)])

    def local(
        leaf_inverse,
        leaf_rhs,
        leaf_tiles,
        mid_inverse_t,
        mid_rhs,
        mid_tiles,
        top_inverse_t,
        top_rhs,
        tile_lists,
    ):
        nb, _, own_rows = mid_inverse_t.shape
        n_top, _, own_top = top_inverse_t.shape
        src = leaf_rhs.shape[2]
        n_z = n_row // n_top

        solved_leaf, swap, update = leaf_stage(
            leaf_inverse[0], leaf_rhs[0], leaf_tiles[0], tile_lists, mid_inverse_t, mid_tiles, n_row
        )

        crossing, staying = [update[half]], [update[0]]
        for k in reversed(range(1, half)):
            crossing.append(row_xor(update[half + k], k))
        for k in range(1, half):
            staying.append(row_xor(update[k], k))
        summed = cross_stage(crossing, nb, own_rows, src)
        crossed = row_xor(summed, half)
        mine, other = resid_stage(staying, crossed, mid_rhs)

        y = lax.axis_index("row") % nb
        swapped = row_xor(swap, 1)
        share = share_stage(top_rhs, n_z)
        shares = [share] + [col_xor(share, dx * CORES) for dx in range(1, n_x)]

        def up(block, have, by):
            pairs = [(i, i + by * nb) for i in range(have * nb, n_row - by * nb)]
            return lax.ppermute(block, "row", pairs)

        given = row_xor(other, 1)
        blocks = [(mine, given)]
        for away in range(1, n_z):
            by = 2 - away % 2
            blocks.append(tuple(up(b, away - by, by) for b in blocks[away - by]))
        own, other, sent = mid_stage(
            blocks, mid_inverse_t, mid_tiles, swapped, n_x, own_top
        )
        sent = col_xor(sent, 1)
        other_own = row_xor(other, 1)
        mid_own = jnp.where(
            y == 0, jnp.stack([own, other_own]), jnp.stack([other_own, own])
        )

        pieces = list(core_stage(own, other, mid_tiles, swapped, sent, n_z))
        for k in range(1, n_z):
            pieces[k] = row_xor(pieces[k], k * n_top)
        part = sum_stage(pieces)
        parts = [part] + [col_xor(part, dx * CORES) for dx in range(1, n_x)]
        own = top_resid_stage(parts, shares)

        mine = top_solve_stage([own, col_xor(own, 1)], top_inverse_t)
        got = [mine] + [row_xor(mine, k * n_top) for k in range(1, n_z)]
        got = [row_xor(piece, k) if k else piece for piece in got for k in range(n_top)]
        spread = narrow_spread if mine.shape[1] % LANES else spread_stage
        top_own = spread(got, n_z, n_top)
        return solved_leaf[None], mid_own, top_own

    return local


def solution(mesh):
    placed = (
        P(("row", "col"), None, None),
        P(("row", "col"), None, None),
        P(("row", "col"), None, None),
        P("col", None, "row"),
        P("col", "row", None),
        P("col", None, "row"),
        P(None, None, "col"),
        P(None, "col", None),
        P(("row", "col"), None),
    )
    return jax.shard_map(
        make_local(mesh.shape["row"], mesh.shape["col"]),
        mesh=mesh,
        in_specs=placed,
        out_specs=(P(("row", "col"), None, None), P("col", "row", None), P(None, "col", None)),
        check_vma=False,
    )
```

time: 325 us -> 102 us (0.31)
  waiting for transfers between devices: 287 us -> 43.9 us
  starting transfers between devices: 0.2 us -> 47.4 us
  between operations: 14.6 us -> 1.49 us
  matrix products: 11.5 us -> 0 us
  Pallas kernels: 0 us -> 7.82 us
  other arithmetic: 6.48 us -> 0.73 us
  local copies, waits for them, and re-layouts: 4.84 us -> 0.03 us
    reduce_scatter x2 -> x0, waiting for transfers between devices: 133 us -> none  [the longest x1 90.4 us: local(): lax.psum_scatter(mid_terms, 'row', scatter_dimension=1, tiled=True)]
    psum x1 -> x0, waiting for transfers between devices: 81.3 us -> none  [local(): summed_rows = lax.psum(top_terms, 'row')]
    all_gather x2 -> x0, waiting for transfers between devices: 72.5 us -> none  [the longest x1 50.8 us: local(): lax.all_gather(mid_resid, 'row', axis=1, tiled=True)]
    ppermute x0 -> x30, starting transfers between devices: none -> 47.4 us  [the longest x20 34.4 us: row_xor(): return lax.ppermute(x, 'row', [(i, i ^ k) for i in range(n_row)])]
    ppermute x0 -> x30, waiting for transfers between devices: none -> 43.9 us  [the longest x20 36.3 us: row_xor(): return lax.ppermute(x, 'row', [(i, i ^ k) for i in range(n_row)])]
    dot_general x5 -> x0, matrix products: 11.5 us -> none  [the longest x2 4.94 us: solve_piece(): lax.dot_general(inverse_cols, piece, (((1,), (1,)), ((0,), (0,))), prefer...]
    pallas_call x0 -> x10, Pallas kernels: none -> 7.82 us  [call(): pl.pallas_call(body, out_shape=[jax.ShapeDtypeStruct(s, BF16) for s in sh...]
    unnamed x16 -> x10, local copies, waits for them, and re-layouts: 4.84 us -> 0.03 us
  transfers between devices with their start and end apart: 5 -> 30, of which waited for: 5 -> 14; matrix products, arithmetic and copies ran while one was open for 0% -> 1% of each run, Pallas kernels for 0% -> 1%
where the time goes in v1:
time: 102 us; the launch traced here: 101 us
  starting transfers between devices  47.4 us (46%)
  waiting for transfers between devices  43.9 us (43%)
  Pallas kernels  7.82 us (8%)
  between operations  1.49 us (1%)
    ppermute x20, waiting for transfers between devices, row_xor(): return lax.ppermute(x, 'row', [(i, i ^ k) for i in range(n_row)])  36.3 us
    ppermute x20, starting transfers between devices, row_xor(): return lax.ppermute(x, 'row', [(i, i ^ k) for i in range(n_row)])  34.4 us
    ppermute x6, starting transfers between devices, up(): return lax.ppermute(block, 'row', pairs)  10.7 us
    pallas_call x10, Pallas kernels, call(): pl.pallas_call(body, out_shape=[jax.ShapeDtypeStruct(s, BF16) for s in sh...  7.82 us
    ppermute x4, waiting for transfers between devices, col_xor(): return lax.ppermute(x, 'col', [(i, i ^ k) for i in range(n_col)])  5.64 us
    ppermute x4, starting transfers between devices, col_xor(): return lax.ppermute(x, 'col', [(i, i ^ k) for i in range(n_col)])  2.3 us
  transfers between devices with their start and end apart: 30, of which 14 were waited for; matrix products, arithmetic and copies ran while one was open for 1% of the time, Pallas kernels for 1%

profile of v1, /device:TPU:0, one launch (start us, length us, event | category | flops | bytes accessed | tf_op | source)
XLA Modules:
  0.0 101.4 jit_solution(15425983107651076520)
XLA Ops:
  1.3 4.5 %shard_map.112 = (bf16[1024,512]{1,0:T(8,128)(2,1)}, bf16[2,1024,128]{2,1,0:T(8,128)(2,1)S(1)}, bf16[528,128]{1,0:T(8,128)(2,1)S(1)}, bf16[528,128]{1,0:T(8,128)...) custom-call(bf16[1024,1024]{1,0:T(8,128)(2,1)} %bitcast.7, ...), custom_call_target="tpu_custom_call" | custom-call | tf_op jit(solution)/shard_map/pallas_call | solution.py:40
  5.8 0.0 copy-start
  5.8 0.0 copy-start.1
  5.8 4.1 %collective-permute-start.3 = (bf16[528,128]{1,0:T(8,128)(2,1)S(1)}, bf16[528,128]{1,0:T(8,128)(2,1)S(1)}, u32[]{:S(2)}, u32[]{:S(2)}) collective-permute-start(bf16[528,128]{1,0:T(8,128)(2,1)S(1)} %get-tuple-element.28), channel_id=1, source_target_pairs={{0,12},{4,8},{8,4},{12,0},{16,28},{20,24},{24,20},{28,16},{1,13},{... | collective-permute-start | bytes 405512 | tf_op jit(solution)/shard_map/ppermute | solution.py:317
  9.9 0.4 collective-permute-start.4
  10.3 0.2 collective-permute-start.5
  10.5 3.8 %collective-permute-done.3.refs_1_ = bf16[528,128]{1,0:T(8,128)(2,1)S(1)} collective-permute-done((bf16[528,128]{1,0:T(8,128)(2,1)S(1)}, bf16[528,128]{1,0:T(8,128)(2,1)S(1)}, u32[]{:S(2)}, u32[]{:S(2)}) %collective-permute-start.3) | collective-permute-done | bytes 135200 | tf_op jit(solution)/shard_map/ppermute | solution.py:317
  14.3 2.2 %collective-permute-done.4.refs_2_ = bf16[528,128]{1,0:T(8,128)(2,1)S(1)} collective-permute-done((bf16[528,128]{1,0:T(8,128)(2,1)S(1)}, bf16[528,128]{1,0:T(8,128)(2,1)S(1)}, u32[]{:S(2)}, u32[]{:S(2)}) %collective-permute-start.4) | collective-permute-done | bytes 135200 | tf_op jit(solution)/shard_map/ppermute | solution.py:317
  16.5 0.0 collective-permute-done.5.refs_3_
  16.5 0.2 shard_map.113
  16.8 2.6 %collective-permute-start.6 = (bf16[256,512]{1,0:T(8,128)(2,1)S(1)}, bf16[256,512]{1,0:T(8,128)(2,1)S(1)}, u32[]{:S(2)}, u32[]{:S(2)}) collective-permute-start(bf16[256,512]{1,0:T(8,128)(2,1)S(1)} %shard_map.113), channel_id=1, source_target_pairs={{0,16},{4,20},{8,24},{12,28},{16,0},{20,4},{24,8},{28,12},{1,17},{... | collective-permute-start | bytes 786440 | tf_op jit(solution)/shard_map/ppermute | solution.py:317
  19.4 1.5 %collective-permute-start = (bf16[528,128]{1,0:T(8,128)(2,1)S(1)}, bf16[528,128]{1,0:T(8,128)(2,1)S(1)}, u32[]{:S(2)}, u32[]{:S(2)}) collective-permute-start(bf16[528,128]{1,0:T(8,128)(2,1)S(1)} %get-tuple-element.24), channel_id=1, source_target_pairs={{0,4},{4,0},{8,12},{12,8},{16,20},{20,16},{24,28},{28,24},{1,5},{5... | collective-permute-start | bytes 405512 | tf_op jit(solution)/shard_map/ppermute | solution.py:317
  20.9 1.6 %collective-permute-start.1 = (bf16[528,128]{1,0:T(8,128)(2,1)S(1)}, bf16[528,128]{1,0:T(8,128)(2,1)S(1)}, u32[]{:S(2)}, u32[]{:S(2)}) collective-permute-start(bf16[528,128]{1,0:T(8,128)(2,1)S(1)} %get-tuple-element.25), channel_id=1, source_target_pairs={{0,8},{4,12},{8,0},{12,4},{16,24},{20,28},{24,16},{28,20},{1,9},{5... | collective-permute-start | bytes 405512 | tf_op jit(solution)/shard_map/ppermute | solution.py:317
  22.4 0.5 collective-permute-start.2
  22.9 1.5 %collective-permute-start.14 = (bf16[2,1024,128]{2,1,0:T(8,128)(2,1)S(1)}, bf16[2,1024,128]{2,1,0:T(8,128)(2,1)S(1)}, u32[]{:S(2)}, u32[]{:S(2)}) collective-permute-start(bf16[2,1024,128]{2,1,0:T(8,128)(2,1)S(1)} %get-tuple-element.33), channel_id=1, source_target_pairs={{0,4},{4,0},{8,12},{12,8},{16,20},{20,16},{24,28},{28,24},{1,5},{5... | collective-permute-start | bytes 1572872 | tf_op jit(solution)/shard_map/ppermute | solution.py:317
  24.4 0.4 collective-permute-done.refs_1_
  24.8 6.9 %collective-permute-done.1.refs_2_ = bf16[528,128]{1,0:T(8,128)(2,1)S(1)} collective-permute-done((bf16[528,128]{1,0:T(8,128)(2,1)S(1)}, bf16[528,128]{1,0:T(8,128)(2,1)S(1)}, u32[]{:S(2)}, u32[]{:S(2)}) %collective-permute-start.1) | collective-permute-done | bytes 135200 | tf_op jit(solution)/shard_map/ppermute | solution.py:317
  31.6 1.9 %collective-permute-done.2.refs_3_ = bf16[528,128]{1,0:T(8,128)(2,1)S(1)} collective-permute-done((bf16[528,128]{1,0:T(8,128)(2,1)S(1)}, bf16[528,128]{1,0:T(8,128)(2,1)S(1)}, u32[]{:S(2)}, u32[]{:S(2)}) %collective-permute-start.2) | collective-permute-done | bytes 135200 | tf_op jit(solution)/shard_map/ppermute | solution.py:317
  33.5 0.0 collective-permute-done.6.refs_4_
  33.5 0.3 shard_map.114
  33.8 1.2 %collective-permute-start.7 = (bf16[128,512]{1,0:T(8,128)(2,1)S(1)}, bf16[128,512]{1,0:T(8,128)(2,1)S(1)}, u32[]{:S(2)}, u32[]{:S(2)}) collective-permute-start(bf16[128,512]{1,0:T(8,128)(2,1)S(1)} %get-tuple-element.32), channel_id=1, source_target_pairs={{0,4},{4,0},{8,12},{12,8},{16,20},{20,16},{24,28},{28,24},{1,5},{5... | collective-permute-start | bytes 393224 | tf_op jit(solution)/shard_map/ppermute | solution.py:317
  35.0 1.7 %collective-permute-start.10 = (bf16[128,512]{1,0:T(8,128)(2,1)S(1)}, bf16[128,512]{1,0:T(8,128)(2,1)S(1)}, u32[]{:S(2)}, u32[]{:S(2)}) collective-permute-start(bf16[128,512]{1,0:T(8,128)(2,1)S(1)} %get-tuple-element.31.refs_0_), channel_id=1, source_target_pairs={{0,16},{4,20},{8,24},{12,28},{1,17},{5,21},{9,25},{13,29},{2,18},{... | collective-permute-start | bytes 393224 | tf_op jit(solution)/shard_map/ppermute | solution.py:358
  36.7 4.7 %collective-permute-done.7.refs_1_ = bf16[128,512]{1,0:T(8,128)(2,1)S(1)} collective-permute-done((bf16[128,512]{1,0:T(8,128)(2,1)S(1)}, bf16[128,512]{1,0:T(8,128)(2,1)S(1)}, u32[]{:S(2)}, u32[]{:S(2)}) %collective-permute-start.7) | collective-permute-done | bytes 131104 | tf_op jit(solution)/shard_map/ppermute | solution.py:317
  41.4 2.2 %collective-permute-start.11 = (bf16[128,512]{1,0:T(8,128)(2,1)S(1)}, bf16[128,512]{1,0:T(8,128)(2,1)S(1)}, u32[]{:S(2)}, u32[]{:S(2)}) collective-permute-start(bf16[128,512]{1,0:T(8,128)(2,1)S(1)} %collective-permute-done.7.refs_1_), channel_id=1, source_target_pairs={{0,16},{4,20},{8,24},{12,28},{1,17},{5,21},{9,25},{13,29},{2,18},{... | collective-permute-start | bytes 393224 | tf_op jit(solution)/shard_map/ppermute | solution.py:358
  43.6 3.5 %collective-permute-start.8 = (bf16[128,512]{1,0:T(8,128)(2,1)S(1)}, bf16[128,512]{1,0:T(8,128)(2,1)S(1)}, u32[]{:S(2)}, u32[]{:S(2)}) collective-permute-start(bf16[128,512]{1,0:T(8,128)(2,1)S(1)} %get-tuple-element.31.refs_0_), channel_id=1, source_target_pairs={{0,8},{4,12},{8,16},{12,20},{16,24},{20,28},{1,9},{5,13},{9,17},{1... | collective-permute-start | bytes 393224 | tf_op jit(solution)/shard_map/ppermute | solution.py:358
  47.1 1.9 %collective-permute-start.9 = (bf16[128,512]{1,0:T(8,128)(2,1)S(1)}, bf16[128,512]{1,0:T(8,128)(2,1)S(1)}, u32[]{:S(2)}, u32[]{:S(2)}) collective-permute-start(bf16[128,512]{1,0:T(8,128)(2,1)S(1)} %collective-permute-done.7.refs_1_), channel_id=1, source_target_pairs={{0,8},{4,12},{8,16},{12,20},{16,24},{20,28},{1,9},{5,13},{9,17},{1... | collective-permute-start | bytes 393224 | tf_op jit(solution)/shard_map/ppermute | solution.py:358
  49.0 0.0 collective-permute-done.10.refs_4_
  49.0 0.7 collective-permute-start.12
  49.7 0.7 collective-permute-start.13
  50.4 0.0 collective-permute-done.14.refs_10_.swap
  50.4 0.5 collective-permute-done.8.refs_2_
  50.9 1.5 %collective-permute-done.9.refs_3_ = bf16[128,512]{1,0:T(8,128)(2,1)S(1)} collective-permute-done((bf16[128,512]{1,0:T(8,128)(2,1)S(1)}, bf16[128,512]{1,0:T(8,128)(2,1)S(1)}, u32[]{:S(2)}, u32[]{:S(2)}) %collective-permute-start.9) | collective-permute-done | bytes 131104 | tf_op jit(solution)/shard_map/ppermute | solution.py:358
  52.4 0.0 collective-permute-done.12.refs_6_
  52.4 0.0 collective-permute-done.13.refs_7_
  52.4 1.0 shard_map.115
  53.4 0.0 copy-start.2
  53.4 0.1 collective-permute-start.16
  53.5 1.9 %collective-permute-done.16.far = bf16[2,256,512]{2,1,0:T(8,128)(2,1)S(1)} collective-permute-done((bf16[2,256,512]{2,1,0:T(8,128)(2,1)S(1)}, bf16[2,256,512]{2,1,0:T(8,128)(2,1)S(1)}, u32[]{:S(2)}, u32[]{:S(2)}) %collective-permute-start.16) | collective-permute-done | bytes 524320 | tf_op jit(solution)/shard_map/ppermute | solution.py:320
  55.4 0.4 shard_map.116
  55.8 2.5 %collective-permute-start.17 = (bf16[512,128]{1,0:T(8,128)(2,1)S(1)}, bf16[512,128]{1,0:T(8,128)(2,1)S(1)}, u32[]{:S(2)}, u32[]{:S(2)}) collective-permute-start(bf16[512,128]{1,0:T(8,128)(2,1)S(1)} %get-tuple-element.38), channel_id=1, source_target_pairs={{0,8},{4,12},{8,0},{12,4},{16,24},{20,28},{24,16},{28,20},{1,9},{5... | collective-permute-start | bytes 393224 | tf_op jit(solution)/shard_map/ppermute | solution.py:317
  58.3 7.3 %collective-permute-start.18 = (bf16[512,128]{1,0:T(8,128)(2,1)S(1)}, bf16[512,128]{1,0:T(8,128)(2,1)S(1)}, u32[]{:S(2)}, u32[]{:S(2)}) collective-permute-start(bf16[512,128]{1,0:T(8,128)(2,1)S(1)} %get-tuple-element.39), channel_id=1, source_target_pairs={{0,16},{4,20},{8,24},{12,28},{16,0},{20,4},{24,8},{28,12},{1,17},{... | collective-permute-start | bytes 393224 | tf_op jit(solution)/shard_map/ppermute | solution.py:317
  65.7 10.0 %collective-permute-done.18.refs_2_ = bf16[512,128]{1,0:T(8,128)(2,1)S(1)} collective-permute-done((bf16[512,128]{1,0:T(8,128)(2,1)S(1)}, bf16[512,128]{1,0:T(8,128)(2,1)S(1)}, u32[]{:S(2)}, u32[]{:S(2)}) %collective-permute-start.18) | collective-permute-done | bytes 131104 | tf_op jit(solution)/shard_map/ppermute | solution.py:317
  75.7 0.1 shard_map.117.refs_0_
  75.7 1.6 %collective-permute-start.20 = (bf16[512,128]{1,0:T(8,128)(2,1)S(1)}, bf16[512,128]{1,0:T(8,128)(2,1)S(1)}, u32[]{:S(2)}, u32[]{:S(2)}) collective-permute-start(bf16[512,128]{1,0:T(8,128)(2,1)S(1)} %shard_map.117.refs_0_), channel_id=1, source_target_pairs={{0,2},{1,3},{2,0},{3,1},{4,6},{5,7},{6,4},{7,5},{8,10},{9,11},{10,... | collective-permute-start | bytes 393224 | tf_op jit(solution)/shard_map/ppermute | solution.py:320
  77.3 0.6 collective-permute-start.21
  77.9 3.7 %collective-permute-done.21.refs_3_ = bf16[256,128]{1,0:T(8,128)(2,1)S(1)} collective-permute-done((bf16[256,128]{1,0:T(8,128)(2,1)S(1)}, bf16[256,128]{1,0:T(8,128)(2,1)S(1)}, u32[]{:S(2)}, u32[]{:S(2)}) %collective-permute-start.21) | collective-permute-done | bytes 65568 | tf_op jit(solution)/shard_map/ppermute | solution.py:320
  81.6 0.0 collective-permute-done.20.refs_1_
  81.6 0.1 shard_map.119.refs_0_
  81.7 0.1 collective-permute-start.22
  81.8 1.7 %collective-permute-start.15 = (bf16[128,512]{1,0:T(8,128)(2,1)S(1)}, bf16[128,512]{1,0:T(8,128)(2,1)S(1)}, u32[]{:S(2)}, u32[]{:S(2)}) collective-permute-start(bf16[128,512]{1,0:T(8,128)(2,1)S(1)} %get-tuple-element.35.other), channel_id=1, source_target_pairs={{0,4},{4,0},{8,12},{12,8},{16,20},{20,16},{24,28},{28,24},{1,5},{5... | collective-permute-start | bytes 393224 | tf_op jit(solution)/shard_map/ppermute | solution.py:317
  83.5 0.0 collective-permute-done.22.refs_1_
  83.5 0.4 shard_map.120.refs_0_
  83.8 2.9 %collective-permute-start.24 = (bf16[256,128]{1,0:T(8,128)(2,1)S(1)}, bf16[256,128]{1,0:T(8,128)(2,1)S(1)}, u32[]{:S(2)}, u32[]{:S(2)}) collective-permute-start(bf16[256,128]{1,0:T(8,128)(2,1)S(1)} %shard_map.120.refs_0_), channel_id=1, source_target_pairs={{0,8},{4,12},{8,0},{12,4},{16,24},{20,28},{24,16},{28,20},{1,9},{5... | collective-permute-start | bytes 196616 | tf_op jit(solution)/shard_map/ppermute | solution.py:317
  86.7 1.1 %collective-permute-start.26 = (bf16[256,128]{1,0:T(8,128)(2,1)S(1)}, bf16[256,128]{1,0:T(8,128)(2,1)S(1)}, u32[]{:S(2)}, u32[]{:S(2)}) collective-permute-start(bf16[256,128]{1,0:T(8,128)(2,1)S(1)} %shard_map.120.refs_0_), channel_id=1, source_target_pairs={{0,16},{4,20},{8,24},{12,28},{16,0},{20,4},{24,8},{28,12},{1,17},{... | collective-permute-start | bytes 196616 | tf_op jit(solution)/shard_map/ppermute | solution.py:317
  87.8 1.4 %collective-permute-start.28 = (bf16[256,128]{1,0:T(8,128)(2,1)S(1)}, bf16[256,128]{1,0:T(8,128)(2,1)S(1)}, u32[]{:S(2)}, u32[]{:S(2)}) collective-permute-start(bf16[256,128]{1,0:T(8,128)(2,1)S(1)} %shard_map.120.refs_0_), channel_id=1, source_target_pairs={{0,24},{4,28},{8,16},{12,20},{16,8},{20,12},{24,0},{28,4},{1,25},{... | collective-permute-start | bytes 196616 | tf_op jit(solution)/shard_map/ppermute | solution.py:317
  89.2 1.3 %collective-permute-start.23 = (bf16[256,128]{1,0:T(8,128)(2,1)S(1)}, bf16[256,128]{1,0:T(8,128)(2,1)S(1)}, u32[]{:S(2)}, u32[]{:S(2)}) collective-permute-start(bf16[256,128]{1,0:T(8,128)(2,1)S(1)} %shard_map.120.refs_0_), channel_id=1, source_target_pairs={{0,4},{4,0},{8,12},{12,8},{16,20},{20,16},{24,28},{28,24},{1,5},{5... | collective-permute-start | bytes 196616 | tf_op jit(solution)/shard_map/ppermute | solution.py:317
  90.4 0.8 collective-permute-start.25
  91.2 3.7 %collective-permute-done.26.refs_4_ = bf16[256,128]{1,0:T(8,128)(2,1)S(1)} collective-permute-done((bf16[256,128]{1,0:T(8,128)(2,1)S(1)}, bf16[256,128]{1,0:T(8,128)(2,1)S(1)}, u32[]{:S(2)}, u32[]{:S(2)}) %collective-permute-start.26) | collective-permute-done | bytes 65568 | tf_op jit(solution)/shard_map/ppermute | solution.py:317
  94.9 1.3 %collective-permute-start.27 = (bf16[256,128]{1,0:T(8,128)(2,1)S(1)}, bf16[256,128]{1,0:T(8,128)(2,1)S(1)}, u32[]{:S(2)}, u32[]{:S(2)}) collective-permute-start(bf16[256,128]{1,0:T(8,128)(2,1)S(1)} %collective-permute-done.26.refs_4_), channel_id=1, source_target_pairs={{0,4},{4,0},{8,12},{12,8},{16,20},{20,16},{24,28},{28,24},{1,5},{5... | collective-permute-start | bytes 196616 | tf_op jit(solution)/shard_map/ppermute | solution.py:317
  96.2 0.8 collective-permute-start.29
  97.0 0.7 maximum_select_fusion
  97.7 1.5 %collective-permute-done.27.refs_5_ = bf16[256,128]{1,0:T(8,128)(2,1)S(1)} collective-permute-done((bf16[256,128]{1,0:T(8,128)(2,1)S(1)}, bf16[256,128]{1,0:T(8,128)(2,1)S(1)}, u32[]{:S(2)}, u32[]{:S(2)}) %collective-permute-start.27) | collective-permute-done | bytes 65568 | tf_op jit(solution)/shard_map/ppermute | solution.py:317
  99.2 1.3 %collective-permute-done.29.refs_7_ = bf16[256,128]{1,0:T(8,128)(2,1)S(1)} collective-permute-done((bf16[256,128]{1,0:T(8,128)(2,1)S(1)}, bf16[256,128]{1,0:T(8,128)(2,1)S(1)}, u32[]{:S(2)}, u32[]{:S(2)}) %collective-permute-start.29) | collective-permute-done | bytes 65568 | tf_op jit(solution)/shard_map/ppermute | solution.py:317
  100.5 0.9 shard_map.121
  (17 shorter events, 0.1 us)
Async XLA Ops:
  1.3 32.3 %copy-start.4 = (bf16[2,128,512]{2,1,0:T(8,128)(2,1)S(1)}, bf16[2,128,512]{2,1,0:T(8,128)(2,1)}, u32[]{:S(2)}) copy-start(bf16[2,128,512]{2,1,0:T(8,128)(2,1)} %refs_5_.1) | copy-start | bytes 786436
  5.8 46.6 %copy-start = (bf16[2,1024,128]{2,1,0:T(8,128)(2,1)S(1)}, bf16[2,1024,128]{2,1,0:T(8,128)(2,1)}, u32[]{:S(2)}) copy-start(bf16[2,1024,128]{2,1,0:T(8,128)(2,1)} %tiles.1) | copy-start | bytes 1572868
  5.8 46.6 %copy-start.1 = (bf16[2,1024,128]{2,1,0:T(8,128)(2,1)S(1)}, bf16[2,1024,128]{2,1,0:T(8,128)(2,1)}, u32[]{:S(2)}) copy-start(bf16[2,1024,128]{2,1,0:T(8,128)(2,1)} %refs_8_.1) | copy-start | bytes 1572868
  5.8 8.5 %collective-permute-start.3 = (bf16[528,128]{1,0:T(8,128)(2,1)S(1)}, bf16[528,128]{1,0:T(8,128)(2,1)S(1)}, u32[]{:S(2)}, u32[]{:S(2)}) collective-permute-start(bf16[528,128]{1,0:T(8,128)(2,1)S(1)} %get-tuple-element.28), channel_id=1, source_target_pairs={{0,12},{4,8},{8,4},{12,0},{16,28},{20,24},{24,20},{28,16},{1,13},{... | collective-permute-start | bytes 405512 | tf_op jit(solution)/shard_map/ppermute | solution.py:317
  9.9 6.6 %collective-permute-start.4 = (bf16[528,128]{1,0:T(8,128)(2,1)S(1)}, bf16[528,128]{1,0:T(8,128)(2,1)S(1)}, u32[]{:S(2)}, u32[]{:S(2)}) collective-permute-start(bf16[528,128]{1,0:T(8,128)(2,1)S(1)} %get-tuple-element.29), channel_id=1, source_target_pairs={{0,8},{4,12},{8,0},{12,4},{16,24},{20,28},{24,16},{28,20},{1,9},{5... | collective-permute-start | bytes 405512 | tf_op jit(solution)/shard_map/ppermute | solution.py:317
  10.3 6.2 %collective-permute-start.5 = (bf16[528,128]{1,0:T(8,128)(2,1)S(1)}, bf16[528,128]{1,0:T(8,128)(2,1)S(1)}, u32[]{:S(2)}, u32[]{:S(2)}) collective-permute-start(bf16[528,128]{1,0:T(8,128)(2,1)S(1)} %get-tuple-element.30), channel_id=1, source_target_pairs={{0,4},{4,0},{8,12},{12,8},{16,20},{20,16},{24,28},{28,24},{1,5},{5... | collective-permute-start | bytes 405512 | tf_op jit(solution)/shard_map/ppermute | solution.py:317
  16.8 16.8 %collective-permute-start.6 = (bf16[256,512]{1,0:T(8,128)(2,1)S(1)}, bf16[256,512]{1,0:T(8,128)(2,1)S(1)}, u32[]{:S(2)}, u32[]{:S(2)}) collective-permute-start(bf16[256,512]{1,0:T(8,128)(2,1)S(1)} %shard_map.113), channel_id=1, source_target_pairs={{0,16},{4,20},{8,24},{12,28},{16,0},{20,4},{24,8},{28,12},{1,17},{... | collective-permute-start | bytes 786440 | tf_op jit(solution)/shard_map/ppermute | solution.py:317
  19.4 5.3 %collective-permute-start = (bf16[528,128]{1,0:T(8,128)(2,1)S(1)}, bf16[528,128]{1,0:T(8,128)(2,1)S(1)}, u32[]{:S(2)}, u32[]{:S(2)}) collective-permute-start(bf16[528,128]{1,0:T(8,128)(2,1)S(1)} %get-tuple-element.24), channel_id=1, source_target_pairs={{0,4},{4,0},{8,12},{12,8},{16,20},{20,16},{24,28},{28,24},{1,5},{5... | collective-permute-start | bytes 405512 | tf_op jit(solution)/shard_map/ppermute | solution.py:317
  20.9 10.7 %collective-permute-start.1 = (bf16[528,128]{1,0:T(8,128)(2,1)S(1)}, bf16[528,128]{1,0:T(8,128)(2,1)S(1)}, u32[]{:S(2)}, u32[]{:S(2)}) collective-permute-start(bf16[528,128]{1,0:T(8,128)(2,1)S(1)} %get-tuple-element.25), channel_id=1, source_target_pairs={{0,8},{4,12},{8,0},{12,4},{16,24},{20,28},{24,16},{28,20},{1,9},{5... | collective-permute-start | bytes 405512 | tf_op jit(solution)/shard_map/ppermute | solution.py:317
  22.4 11.1 %collective-permute-start.2 = (bf16[528,128]{1,0:T(8,128)(2,1)S(1)}, bf16[528,128]{1,0:T(8,128)(2,1)S(1)}, u32[]{:S(2)}, u32[]{:S(2)}) collective-permute-start(bf16[528,128]{1,0:T(8,128)(2,1)S(1)} %get-tuple-element.26), channel_id=1, source_target_pairs={{0,12},{4,8},{8,4},{12,0},{16,28},{20,24},{24,20},{28,16},{1,13},{... | collective-permute-start | bytes 405512 | tf_op jit(solution)/shard_map/ppermute | solution.py:317
  22.9 27.5 %collective-permute-start.14 = (bf16[2,1024,128]{2,1,0:T(8,128)(2,1)S(1)}, bf16[2,1024,128]{2,1,0:T(8,128)(2,1)S(1)}, u32[]{:S(2)}, u32[]{:S(2)}) collective-permute-start(bf16[2,1024,128]{2,1,0:T(8,128)(2,1)S(1)} %get-tuple-element.33), channel_id=1, source_target_pairs={{0,4},{4,0},{8,12},{12,8},{16,20},{20,16},{24,28},{28,24},{1,5},{5... | collective-permute-start | bytes 1572872 | tf_op jit(solution)/shard_map/ppermute | solution.py:317
  33.8 7.6 %collective-permute-start.7 = (bf16[128,512]{1,0:T(8,128)(2,1)S(1)}, bf16[128,512]{1,0:T(8,128)(2,1)S(1)}, u32[]{:S(2)}, u32[]{:S(2)}) collective-permute-start(bf16[128,512]{1,0:T(8,128)(2,1)S(1)} %get-tuple-element.32), channel_id=1, source_target_pairs={{0,4},{4,0},{8,12},{12,8},{16,20},{20,16},{24,28},{28,24},{1,5},{5... | collective-permute-start | bytes 393224 | tf_op jit(solution)/shard_map/ppermute | solution.py:317
  35.0 42.3 %copy-start.3 = (bf16[2,256,512]{2,1,0:T(8,128)(2,1)S(1)}, bf16[2,256,512]{2,1,0:T(8,128)(2,1)}, u32[]{:S(2)}) copy-start(bf16[2,256,512]{2,1,0:T(8,128)(2,1)} %rhs.1) | copy-start | bytes 1572868
  35.0 14.1 %collective-permute-start.10 = (bf16[128,512]{1,0:T(8,128)(2,1)S(1)}, bf16[128,512]{1,0:T(8,128)(2,1)S(1)}, u32[]{:S(2)}, u32[]{:S(2)}) collective-permute-start(bf16[128,512]{1,0:T(8,128)(2,1)S(1)} %get-tuple-element.31.refs_0_), channel_id=1, source_target_pairs={{0,16},{4,20},{8,24},{12,28},{1,17},{5,21},{9,25},{13,29},{2,18},{... | collective-permute-start | bytes 393224 | tf_op jit(solution)/shard_map/ppermute | solution.py:358
  41.4 8.4 %collective-permute-start.11 = (bf16[128,512]{1,0:T(8,128)(2,1)S(1)}, bf16[128,512]{1,0:T(8,128)(2,1)S(1)}, u32[]{:S(2)}, u32[]{:S(2)}) collective-permute-start(bf16[128,512]{1,0:T(8,128)(2,1)S(1)} %collective-permute-done.7.refs_1_), channel_id=1, source_target_pairs={{0,16},{4,20},{8,24},{12,28},{1,17},{5,21},{9,25},{13,29},{2,18},{... | collective-permute-start | bytes 393224 | tf_op jit(solution)/shard_map/ppermute | solution.py:358
  43.6 7.3 %collective-permute-start.8 = (bf16[128,512]{1,0:T(8,128)(2,1)S(1)}, bf16[128,512]{1,0:T(8,128)(2,1)S(1)}, u32[]{:S(2)}, u32[]{:S(2)}) collective-permute-start(bf16[128,512]{1,0:T(8,128)(2,1)S(1)} %get-tuple-element.31.refs_0_), channel_id=1, source_target_pairs={{0,8},{4,12},{8,16},{12,20},{16,24},{20,28},{1,9},{5,13},{9,17},{1... | collective-permute-start | bytes 393224 | tf_op jit(solution)/shard_map/ppermute | solution.py:358
  47.1 5.3 %collective-permute-start.9 = (bf16[128,512]{1,0:T(8,128)(2,1)S(1)}, bf16[128,512]{1,0:T(8,128)(2,1)S(1)}, u32[]{:S(2)}, u32[]{:S(2)}) collective-permute-start(bf16[128,512]{1,0:T(8,128)(2,1)S(1)} %collective-permute-done.7.refs_1_), channel_id=1, source_target_pairs={{0,8},{4,12},{8,16},{12,20},{16,24},{20,28},{1,9},{5,13},{9,17},{1... | collective-permute-start | bytes 393224 | tf_op jit(solution)/shard_map/ppermute | solution.py:358
  49.0 3.3 %collective-permute-start.12 = (bf16[128,512]{1,0:T(8,128)(2,1)S(1)}, bf16[128,512]{1,0:T(8,128)(2,1)S(1)}, u32[]{:S(2)}, u32[]{:S(2)}) collective-permute-start(bf16[128,512]{1,0:T(8,128)(2,1)S(1)} %collective-permute-done.10.refs_4_), channel_id=1, source_target_pairs={{16,24},{20,28},{17,25},{21,29},{18,26},{22,30},{19,27},{23,31}} | collective-permute-start | bytes 393224 | tf_op jit(solution)/shard_map/ppermute | solution.py:358
  49.7 2.6 %collective-permute-start.13 = (bf16[128,512]{1,0:T(8,128)(2,1)S(1)}, bf16[128,512]{1,0:T(8,128)(2,1)S(1)}, u32[]{:S(2)}, u32[]{:S(2)}) collective-permute-start(bf16[128,512]{1,0:T(8,128)(2,1)S(1)} %collective-permute-done.11.refs_5_), channel_id=1, source_target_pairs={{16,24},{20,28},{17,25},{21,29},{18,26},{22,30},{19,27},{23,31}} | collective-permute-start | bytes 393224 | tf_op jit(solution)/shard_map/ppermute | solution.py:358
  53.4 30.0 %copy-start.2 = (bf16[2,1024,256]{2,1,0:T(8,128)(2,1)S(1)}, bf16[2,1024,256]{2,1,0:T(8,128)(2,1)}, u32[]{:S(2)}) copy-start(bf16[2,1024,256]{2,1,0:T(8,128)(2,1)} %refs_2_.1) | copy-start | bytes 3145732
  53.4 2.0 %collective-permute-start.16 = (bf16[2,256,512]{2,1,0:T(8,128)(2,1)S(1)}, bf16[2,256,512]{2,1,0:T(8,128)(2,1)S(1)}, u32[]{:S(2)}, u32[]{:S(2)}) collective-permute-start(bf16[2,256,512]{2,1,0:T(8,128)(2,1)S(1)} %get-tuple-element.36), channel_id=1, source_target_pairs={{0,1},{1,0},{2,3},{3,2},{4,5},{5,4},{6,7},{7,6},{8,9},{9,8},{10,11... | collective-permute-start | bytes 1572872 | tf_op jit(solution)/shard_map/ppermute | solution.py:320
  55.8 9.9 %collective-permute-start.17 = (bf16[512,128]{1,0:T(8,128)(2,1)S(1)}, bf16[512,128]{1,0:T(8,128)(2,1)S(1)}, u32[]{:S(2)}, u32[]{:S(2)}) collective-permute-start(bf16[512,128]{1,0:T(8,128)(2,1)S(1)} %get-tuple-element.38), channel_id=1, source_target_pairs={{0,8},{4,12},{8,0},{12,4},{16,24},{20,28},{24,16},{28,20},{1,9},{5... | collective-permute-start | bytes 393224 | tf_op jit(solution)/shard_map/ppermute | solution.py:317
  58.3 17.3 %collective-permute-start.18 = (bf16[512,128]{1,0:T(8,128)(2,1)S(1)}, bf16[512,128]{1,0:T(8,128)(2,1)S(1)}, u32[]{:S(2)}, u32[]{:S(2)}) collective-permute-start(bf16[512,128]{1,0:T(8,128)(2,1)S(1)} %get-tuple-element.39), channel_id=1, source_target_pairs={{0,16},{4,20},{8,24},{12,28},{16,0},{20,4},{24,8},{28,12},{1,17},{... | collective-permute-start | bytes 393224 | tf_op jit(solution)/shard_map/ppermute | solution.py:317
  65.7 10.0 %collective-permute-start.19 = (bf16[512,128]{1,0:T(8,128)(2,1)S(1)}, bf16[512,128]{1,0:T(8,128)(2,1)S(1)}, u32[]{:S(2)}, u32[]{:S(2)}) collective-permute-start(bf16[512,128]{1,0:T(8,128)(2,1)S(1)} %get-tuple-element.40), channel_id=1, source_target_pairs={{0,24},{4,28},{8,16},{12,20},{16,8},{20,12},{24,0},{28,4},{1,25},{... | collective-permute-start | bytes 393224 | tf_op jit(solution)/shard_map/ppermute | solution.py:317
  75.7 5.9 %collective-permute-start.20 = (bf16[512,128]{1,0:T(8,128)(2,1)S(1)}, bf16[512,128]{1,0:T(8,128)(2,1)S(1)}, u32[]{:S(2)}, u32[]{:S(2)}) collective-permute-start(bf16[512,128]{1,0:T(8,128)(2,1)S(1)} %shard_map.117.refs_0_), channel_id=1, source_target_pairs={{0,2},{1,3},{2,0},{3,1},{4,6},{5,7},{6,4},{7,5},{8,10},{9,11},{10,... | collective-permute-start | bytes 393224 | tf_op jit(solution)/shard_map/ppermute | solution.py:320
  77.3 4.3 %collective-permute-start.21 = (bf16[256,128]{1,0:T(8,128)(2,1)S(1)}, bf16[256,128]{1,0:T(8,128)(2,1)S(1)}, u32[]{:S(2)}, u32[]{:S(2)}) collective-permute-start(bf16[256,128]{1,0:T(8,128)(2,1)S(1)} %shard_map.118.refs_2_), channel_id=1, source_target_pairs={{0,2},{1,3},{2,0},{3,1},{4,6},{5,7},{6,4},{7,5},{8,10},{9,11},{10,... | collective-permute-start | bytes 196616 | tf_op jit(solution)/shard_map/ppermute | solution.py:320
  81.7 1.7 %collective-permute-start.22 = (bf16[512,128]{1,0:T(8,128)(2,1)S(1)}, bf16[512,128]{1,0:T(8,128)(2,1)S(1)}, u32[]{:S(2)}, u32[]{:S(2)}) collective-permute-start(bf16[512,128]{1,0:T(8,128)(2,1)S(1)} %shard_map.119.refs_0_), channel_id=1, source_target_pairs={{0,1},{1,0},{2,3},{3,2},{4,5},{5,4},{6,7},{7,6},{8,9},{9,8},{10,11... | collective-permute-start | bytes 393224 | tf_op jit(solution)/shard_map/ppermute | solution.py:320
  81.8 15.2 %collective-permute-start.15 = (bf16[128,512]{1,0:T(8,128)(2,1)S(1)}, bf16[128,512]{1,0:T(8,128)(2,1)S(1)}, u32[]{:S(2)}, u32[]{:S(2)}) collective-permute-start(bf16[128,512]{1,0:T(8,128)(2,1)S(1)} %get-tuple-element.35.other), channel_id=1, source_target_pairs={{0,4},{4,0},{8,12},{12,8},{16,20},{20,16},{24,28},{28,24},{1,5},{5... | collective-permute-start | bytes 393224 | tf_op jit(solution)/shard_map/ppermute | solution.py:317
  83.8 6.6 %collective-permute-start.24 = (bf16[256,128]{1,0:T(8,128)(2,1)S(1)}, bf16[256,128]{1,0:T(8,128)(2,1)S(1)}, u32[]{:S(2)}, u32[]{:S(2)}) collective-permute-start(bf16[256,128]{1,0:T(8,128)(2,1)S(1)} %shard_map.120.refs_0_), channel_id=1, source_target_pairs={{0,8},{4,12},{8,0},{12,4},{16,24},{20,28},{24,16},{28,20},{1,9},{5... | collective-permute-start | bytes 196616 | tf_op jit(solution)/shard_map/ppermute | solution.py:317
  86.7 8.2 %collective-permute-start.26 = (bf16[256,128]{1,0:T(8,128)(2,1)S(1)}, bf16[256,128]{1,0:T(8,128)(2,1)S(1)}, u32[]{:S(2)}, u32[]{:S(2)}) collective-permute-start(bf16[256,128]{1,0:T(8,128)(2,1)S(1)} %shard_map.120.refs_0_), channel_id=1, source_target_pairs={{0,16},{4,20},{8,24},{12,28},{16,0},{20,4},{24,8},{28,12},{1,17},{... | collective-permute-start | bytes 196616 | tf_op jit(solution)/shard_map/ppermute | solution.py:317
  87.8 8.4 %collective-permute-start.28 = (bf16[256,128]{1,0:T(8,128)(2,1)S(1)}, bf16[256,128]{1,0:T(8,128)(2,1)S(1)}, u32[]{:S(2)}, u32[]{:S(2)}) collective-permute-start(bf16[256,128]{1,0:T(8,128)(2,1)S(1)} %shard_map.120.refs_0_), channel_id=1, source_target_pairs={{0,24},{4,28},{8,16},{12,20},{16,8},{20,12},{24,0},{28,4},{1,25},{... | collective-permute-start | bytes 196616 | tf_op jit(solution)/shard_map/ppermute | solution.py:317
  89.2 8.5 %collective-permute-start.23 = (bf16[256,128]{1,0:T(8,128)(2,1)S(1)}, bf16[256,128]{1,0:T(8,128)(2,1)S(1)}, u32[]{:S(2)}, u32[]{:S(2)}) collective-permute-start(bf16[256,128]{1,0:T(8,128)(2,1)S(1)} %shard_map.120.refs_0_), channel_id=1, source_target_pairs={{0,4},{4,0},{8,12},{12,8},{16,20},{20,16},{24,28},{28,24},{1,5},{5... | collective-permute-start | bytes 196616 | tf_op jit(solution)/shard_map/ppermute | solution.py:317
  90.4 7.2 %collective-permute-start.25 = (bf16[256,128]{1,0:T(8,128)(2,1)S(1)}, bf16[256,128]{1,0:T(8,128)(2,1)S(1)}, u32[]{:S(2)}, u32[]{:S(2)}) collective-permute-start(bf16[256,128]{1,0:T(8,128)(2,1)S(1)} %collective-permute-done.24.refs_2_), channel_id=1, source_target_pairs={{0,4},{4,0},{8,12},{12,8},{16,20},{20,16},{24,28},{28,24},{1,5},{5... | collective-permute-start | bytes 196616 | tf_op jit(solution)/shard_map/ppermute | solution.py:317
  94.9 4.3 %collective-permute-start.27 = (bf16[256,128]{1,0:T(8,128)(2,1)S(1)}, bf16[256,128]{1,0:T(8,128)(2,1)S(1)}, u32[]{:S(2)}, u32[]{:S(2)}) collective-permute-start(bf16[256,128]{1,0:T(8,128)(2,1)S(1)} %collective-permute-done.26.refs_4_), channel_id=1, source_target_pairs={{0,4},{4,0},{8,12},{12,8},{16,20},{20,16},{24,28},{28,24},{1,5},{5... | collective-permute-start | bytes 196616 | tf_op jit(solution)/shard_map/ppermute | solution.py:317
  96.2 4.3 %collective-permute-start.29 = (bf16[256,128]{1,0:T(8,128)(2,1)S(1)}, bf16[256,128]{1,0:T(8,128)(2,1)S(1)}, u32[]{:S(2)}, u32[]{:S(2)}) collective-permute-start(bf16[256,128]{1,0:T(8,128)(2,1)S(1)} %collective-permute-done.28.refs_6_), channel_id=1, source_target_pairs={{0,4},{4,0},{8,12},{12,8},{16,20},{20,16},{24,28},{28,24},{1,5},{5... | collective-permute-start | bytes 196616 | tf_op jit(solution)/shard_map/ppermute | solution.py:317
